TPU v7x, 32 devices: a whole 2x2x4 slice. The times are simulated.
32 devices in a mesh: fsdp: 2 (over x), rep: 16 (over z, y, core).
Axes of the slice: x: 2, y: 2, z: 4, core: 2. Of those that a mesh axis runs over, the one named last changes fastest.
Arguments:
- images: bfloat16 [128, 197, 384], P(('fsdp', 'rep')), may hold values from -5 to 5
- cotangent: bfloat16 [128, 197, 384], P(('fsdp', 'rep')), may hold values from -6 to 6
- weights: float32 [1777664], P('fsdp'), may hold values from -3 to 3
- first_moment: float32 [1777664], P(('fsdp', 'rep'))
- second_moment: float32 [1777664], P(('fsdp', 'rep')), as said below
Outputs:
- output: bfloat16 [128, 197, 384], P(('fsdp', 'rep'))
- input_grad: bfloat16 [128, 197, 384], P(('fsdp', 'rep'))
- new_weights: float32 [1777664], P('fsdp')
- gradients: float32 [1777664], P(('fsdp', 'rep'))
- new_first: float32 [1777664], P(('fsdp', 'rep'))
- new_second: float32 [1777664], P(('fsdp', 'rep'))
Inputs may be any that keep to these rules, and one draw needn't show every extreme that they name: second_moment is positive.
All inputs are finite; a program needn't handle non-finite values.
Results may differ from a plain program's by a relative error of at most 0.0095.
The roundings to bfloat16 on the way count: a program that leaves them out, or rounds other values in their place, can miss the bound.
Values may be sent and summed in bfloat16 or wider, within the bound.
A program may use at most 128 MiB of HBM per device.

v0:
```python
import jax
import jax.numpy as jnp
from jax import lax
from jax.sharding import PartitionSpec as P

D = 384
H = 6
FF = 1536
norm_eps = 1e-06
half_root = 0.7071067811865476
inv_root_two_pi = 0.3989422804014327
beta_one = 0.9
beta_two = 0.999
learn_rate = 0.02
decay_rate = 0.05
adam_eps = 1e-08


def product(form, left, right):
    return jnp.einsum(form, left, right, preferred_element_type=jnp.float32)


def layer_norm_forward(values):
    centred = values - jnp.mean(values, -1, keepdims=True)
    variance = jnp.mean(centred * centred, -1, keepdims=True)
    inverse = lax.rsqrt(variance + norm_eps)
    return (centred * inverse, inverse)


def layer_norm_backward(d_scaled, scaled, inverse):
    first_mean = jnp.mean(d_scaled, -1, keepdims=True)
    second_mean = jnp.mean(d_scaled * scaled, -1, keepdims=True)
    return (d_scaled - first_mean - scaled * second_mean) * inverse


def unpack(flat_vec):
    edge_one = 3 * D * D
    edge_two = edge_one + D * D
    edge_three = edge_two + D * FF
    edge_four = edge_three + FF * D
    edge_five = edge_four + 8 * D
    w_qkv = flat_vec[:edge_one].reshape(D, 3 * D)
    w_proj = flat_vec[edge_one:edge_two].reshape(D, D)
    w_fc1 = flat_vec[edge_two:edge_three].reshape(D, FF)
    w_fc2 = flat_vec[edge_three:edge_four].reshape(FF, D)
    vectors = flat_vec[edge_four:edge_five].reshape(8, D)
    b_fc1 = flat_vec[edge_five : edge_five + FF]
    return (w_qkv, w_proj, w_fc1, w_fc2, vectors, b_fc1)


def pack(grads, length):
    pieces = [grad.reshape(-1) for grad in grads]
    used = sum((piece_arr.shape[0] for piece_arr in pieces))
    pieces.append(jnp.zeros((length - used,), jnp.float32))
    return jnp.concatenate(pieces)


def layer_block(images, cotangent, fwd_params, bwd_params):
    w_qkv, w_proj, w_fc1, w_fc2, vectors, b_fc1 = fwd_params
    back_qkv, back_proj, back_fc1, back_fc2, back_vectors, back_b1 = bwd_params
    batch, length, width = images.shape
    head_size = width // H
    token_rows = batch * length
    scale = head_size ** (-0.5)
    vector_float = vectors.astype(jnp.float32)
    backward_vector_slice = back_vectors.astype(jnp.float32)
    input_token_rows = images.astype(jnp.float32).reshape(token_rows, width)
    first_centered_scaled, first_inverse_deviation = layer_norm_forward(input_token_rows)
    first_normed_rows = (first_centered_scaled * vector_float[0] + vector_float[1]).astype(
        jnp.bfloat16
    )
    qkv_rows = jnp.dot(first_normed_rows, w_qkv, preferred_element_type=jnp.float32)
    query = (
        (qkv_rows[:, :width] + vector_float[2])
        .astype(jnp.bfloat16)
        .reshape(batch, length, H, head_size)
    )
    key_arr = (
        qkv_rows[:, width : 2 * width].astype(jnp.bfloat16).reshape(batch, length, H, head_size)
    )
    value = (
        (qkv_rows[:, 2 * width :] + vector_float[3])
        .astype(jnp.bfloat16)
        .reshape(batch, length, H, head_size)
    )
    scores = product("bqhd,bkhd->bhqk", query, key_arr) * scale
    top_score = jnp.max(scores, -1, keepdims=True)
    log_total = top_score + jnp.log(jnp.sum(jnp.exp(scores - top_score), -1, keepdims=True))
    probs_bf = jnp.exp(scores - log_total).astype(jnp.bfloat16)
    mixed = (
        product("bhqk,bkhd->bqhd", probs_bf, value).astype(jnp.bfloat16).reshape(token_rows, width)
    )
    residual_stream = (
        input_token_rows
        + jnp.dot(mixed, w_proj, preferred_element_type=jnp.float32)
        + vector_float[4]
    )
    second_centered_scaled, second_inverse_deviation = layer_norm_forward(residual_stream)
    second_normed_rows = (second_centered_scaled * vector_float[5] + vector_float[6]).astype(
        jnp.bfloat16
    )
    preact = jnp.dot(second_normed_rows, w_fc1, preferred_element_type=jnp.float32) + b_fc1.astype(
        jnp.float32
    )
    normal_cdf = 0.5 * (1.0 + jax.scipy.special.erf(preact * half_root))
    activ = (preact * normal_cdf).astype(jnp.bfloat16)
    result = (
        residual_stream
        + jnp.dot(activ, w_fc2, preferred_element_type=jnp.float32)
        + vector_float[7]
    )
    d_out = cotangent.reshape(token_rows, width)
    output_gradient_float = d_out.astype(jnp.float32)
    grad_fc2 = jnp.dot(activ.T, d_out, preferred_element_type=jnp.float32)
    grad_bias2 = jnp.sum(output_gradient_float, 0)
    d_act = jnp.dot(d_out, back_fc2.T, preferred_element_type=jnp.float32)
    d_pre = d_act * (normal_cdf + preact * jnp.exp(-0.5 * preact * preact) * inv_root_two_pi)
    grad_bias1 = jnp.sum(d_pre, 0)
    d_pre_bf = d_pre.astype(jnp.bfloat16)
    grad_fc1 = jnp.dot(second_normed_rows.T, d_pre_bf, preferred_element_type=jnp.float32)
    second_norm_gradient = jnp.dot(d_pre_bf, back_fc1.T, preferred_element_type=jnp.float32)
    gain2_gradient = jnp.sum(second_norm_gradient * second_centered_scaled, 0)
    grad_shift2 = jnp.sum(second_norm_gradient, 0)
    residual_gradient = output_gradient_float + layer_norm_backward(
        second_norm_gradient * backward_vector_slice[5],
        second_centered_scaled,
        second_inverse_deviation,
    )
    grad_pbias = jnp.sum(residual_gradient, 0)
    d_resid_bf = residual_gradient.astype(jnp.bfloat16)
    grad_proj = jnp.dot(mixed.T, d_resid_bf, preferred_element_type=jnp.float32)
    d_mixed = jnp.dot(d_resid_bf, back_proj.T, preferred_element_type=jnp.float32)
    d_mixed = d_mixed.astype(jnp.bfloat16).reshape(batch, length, H, head_size)
    scores_again = product("bqhd,bkhd->bhqk", query, key_arr) * scale
    probs_full = jnp.exp(scores_again - log_total)
    probs_again = probs_full.astype(jnp.bfloat16)
    d_probs = product("bqhd,bkhd->bhqk", d_mixed, value)
    d_value = product("bhqk,bqhd->bkhd", probs_again, d_mixed).reshape(token_rows, width)
    delta = jnp.sum(probs_full * d_probs, -1, keepdims=True)
    d_scores = (probs_full * (d_probs - delta) * scale).astype(jnp.bfloat16)
    d_query = product("bhqk,bkhd->bqhd", d_scores, key_arr).reshape(token_rows, width)
    d_key = product("bhqk,bqhd->bkhd", d_scores, query).reshape(token_rows, width)
    grad_qbias = jnp.sum(d_query, 0)
    grad_vbias = jnp.sum(d_value, 0)
    d_qkv = jnp.concatenate([d_query, d_key, d_value], 1).astype(jnp.bfloat16)
    grad_qkv = jnp.dot(first_normed_rows.T, d_qkv, preferred_element_type=jnp.float32)
    first_norm_gradient = jnp.dot(d_qkv, back_qkv.T, preferred_element_type=jnp.float32)
    gain1_gradient = jnp.sum(first_norm_gradient * first_centered_scaled, 0)
    grad_shift1 = jnp.sum(first_norm_gradient, 0)
    input_gradient = residual_gradient + layer_norm_backward(
        first_norm_gradient * backward_vector_slice[0],
        first_centered_scaled,
        first_inverse_deviation,
    )
    grad_vectors = jnp.stack(
        [
            gain1_gradient,
            grad_shift1,
            grad_qbias,
            grad_vbias,
            grad_pbias,
            gain2_gradient,
            grad_shift2,
            grad_bias2,
        ]
    )
    grads = (grad_qkv, grad_proj, grad_fc1, grad_fc2, grad_vectors, grad_bias1)
    out_block = result.astype(jnp.bfloat16).reshape(batch, length, width)
    input_block = input_gradient.astype(jnp.bfloat16).reshape(batch, length, width)
    return (out_block, input_block, grads)


def adamw(weight_vals, grad_vals, first_vals, second_vals):
    first_new = beta_one * first_vals + (1.0 - beta_one) * grad_vals
    second_new = beta_two * second_vals + (1.0 - beta_two) * grad_vals * grad_vals
    first_hat = first_new / (1.0 - beta_one**2)
    second_hat = second_new / (1.0 - beta_two**2)
    updated = weight_vals - learn_rate * (
        first_hat / (jnp.sqrt(second_hat) + adam_eps) + decay_rate * weight_vals
    )
    return (updated, first_new, second_new)


def on_device(images, cotangent, weights, first_moment, second_moment):
    half_bf = weights.astype(jnp.bfloat16)
    params = unpack(lax.all_gather(half_bf, "fsdp", axis=0, tiled=True))
    back_params = unpack(lax.all_gather(half_bf, "fsdp", axis=0, tiled=True))
    output, input_grad, grads = layer_block(images, cotangent, params, back_params)
    flat_grad = pack(grads, 2 * weights.shape[0])
    half_grad = lax.psum_scatter(
        flat_grad.astype(jnp.bfloat16), "fsdp", scatter_dimension=0, tiled=True
    ).astype(jnp.float32)
    piece_len = first_moment.shape[0]
    offset = lax.axis_index("rep") * piece_len
    summed_all = lax.psum(half_grad, "rep")
    own_grad = lax.dynamic_slice_in_dim(summed_all, offset, piece_len)
    own_weights = lax.dynamic_slice_in_dim(weights, offset, piece_len)
    new_own, new_first, new_second = adamw(own_weights, own_grad, first_moment, second_moment)
    new_weights = lax.all_gather(new_own, "rep", axis=0, tiled=True)
    return (output, input_grad, new_weights, own_grad, new_first, new_second)


def solution(mesh):
    in_specs = (
        P(("fsdp", "rep"), None, None),
        P(("fsdp", "rep"), None, None),
        P("fsdp"),
        P(("fsdp", "rep")),
        P(("fsdp", "rep")),
    )
    out_specs = (
        P(("fsdp", "rep"), None, None),
        P(("fsdp", "rep"), None, None),
        P("fsdp"),
        P(("fsdp", "rep")),
        P(("fsdp", "rep")),
        P(("fsdp", "rep")),
    )
    return jax.shard_map(
        on_device, mesh=mesh, in_specs=in_specs, out_specs=out_specs, check_vma=False
    )
```

profile of v0, /device:TPU:0, one launch (start us, length us, event | category | flops | bytes accessed | tf_op | source)
XLA Modules:
  0.0 480.9 jit_solution(8858606511135499291)
XLA Ops:
  7.2 3.4 convert_element_type.75
  18.8 44.2 %all-gather.4.cloned.1.call-done = bf16[1777664]{0:T(1024)(128)(2,1)} async-done(((bf16[888832]{0:T(1024)(128)(2,1)}), bf16[1777664]{0:T(1024)(128)(2,1)}) %all-gather.4.cloned.1.call-update) | async-done | bytes 3555344 | tf_op jit(solution)/shard_map/all_gather | solution.py:186
  70.1 2.8 fusion.60
  72.9 3.4 reshape.210
  86.0 3.3 reshape.228
  89.2 2.7 copy.91
  102.6 2.7 reshape.207
  107.7 4.7 multiply_convert_fusion.1
  112.4 16.3 %fusion.65 = (bf16[1536]{0:T(1024)(128)(2,1)}, bf16[788,1536]{1,0:T(8,128)(2,1)S(1)}) fusion(f32[788,1536]{1,0:T(8,128)S(1)} %get-tuple-element.61, f32[1536]{0:T(1024)S(1)} %slice_convert_fusion.2, bf16[788,384]{1,0:T(8,128)(2,1)S(1)} %copy-done.13, bf16[1536,384]{1,0:T(8,128)(2,1)S(1)} %copy-done.18), kind=kOutput, calls=%fused_computation.106 | convolution fusion | flops 944085504 | bytes 9056256 | tf_op jit(solution)/shard_map/dot_general | solution.py:116
  137.4 3.0 reshape.229
  143.1 5.1 %bitcast_convert_fusion = (bf16[4,197,6,64]{1,3,2,0:T(8,128)(2,1)}, f32[4,6,64,197]{3,2,1,0:T(8,128)}) fusion(bf16[4,197,6,64]{1,3,2,0:T(8,128)(2,1)} %copy.97, f32[4,6,197,197]{2,3,1,0:T(8,128)} %copy-done, f32[4,6,197]{2,1,0:T(8,128)S(1)} %log_add_fusion), kind=kOutput, calls=%fused_computation.27 | convolution fusion | flops 122318088 | bytes 6165312 | tf_op jit(solution)/shard_map/bhqk,bqhd->bkhd/dot_general | solution.py:20
  148.2 3.1 fusion.67
  151.3 10.3 %fusion.31 = bf16[4,197,6,64]{1,3,2,0:T(8,128)(2,1)} fusion(bf16[4,197,6,64]{1,3,2,0:T(8,128)(2,1)} %copy-done.11, f32[4,6,197,197]{2,3,1,0:T(8,128)} %fusion.67, f32[4,6,197,197]{2,3,1,0:T(8,128)} %copy-done, f32[4,6,197]{2,1,0:T(8,128)S(1)} %log_add_fusion), kind=kOutput, calls=%fused_computation.39 | convolution fusion | flops 127911504 | bytes 8680608 | tf_op jit(solution)/shard_map/bhqk,bqhd->bkhd/dot_general | solution.py:20
  161.6 10.5 %bitcast_convert_fusion.1 = (bf16[4,197,6,64]{1,3,2,0:T(8,128)(2,1)}, f32[4,6,64,197]{3,2,1,0:T(8,128)}) fusion(bf16[4,197,6,64]{1,3,2,0:T(8,128)(2,1)S(1)} %copy-done.12, f32[4,6,197,197]{2,3,1,0:T(8,128)} %fusion.67, f32[4,6,197,197]{2,3,1,0:T(8,128)} %copy-done, f32[4,6,197]{2,1,0:T(8,128)S(1)} %log_add_fusion), kind=kOutput, calls=%fused_computation.29 | convolution fusion | flops 127911504 | bytes 9890976 | tf_op jit(solution)/shard_map/bhqk,bkhd->bqhd/dot_general | solution.py:20
  185.5 2.8 multiply_reduce_fusion.3
  190.9 2.8 convolution_convert_fusion
  193.8 3.1 reshape.221
  196.9 3.5 reshape.220
  216.4 93.6 %all-reduce.6.cloned.1.call-done = bf16[1777664]{0:T(1024)(128)(2,1)} async-done(((bf16[1777664]{0:T(1024)(128)(2,1)}), bf16[1777664]{0:T(1024)(128)(2,1)}) %all-reduce.6.cloned.1.call-update) | async-done | bytes 3555344
  310.0 3.5 dynamic-slice_convert_fusion
  313.6 107.2 %all-reduce.4.cloned.1.call-done = f32[888832]{0:T(1024)} async-done(((f32[888832]{0:T(1024)}), f32[888832]{0:T(1024)}) %all-reduce.4.cloned.1.call-update) | async-done | bytes 3555344 | tf_op jit(solution)/shard_map/psum | solution.py:195
  423.7 4.3 fusion.29
  432.6 37.5 %all-gather.6.cloned.1.call-done = f32[16,1,55552]{2,1,0:T(1,128)} async-done(((f32[1,1,55552]{2,1,0:T(1,128)}), f32[16,1,55552]{2,1,0:T(1,128)}) %all-gather.6.cloned.1.call-update) | async-done | bytes 3555344 | tf_op jit(solution)/shard_map/all_gather | solution.py:199
  470.1 4.0 copy.135
  (168 shorter events, 87.9 us)
Async XLA Ops:
  7.2 55.9 %all-gather.4.cloned.1.call-start = ((), (), s32[]{:S(2)}) async-start(), calls=%async_computation | async-start | bytes 5332992 | tf_op jit(solution)/shard_map/all_gather | solution.py:186
  10.6 299.4 %all-reduce.6.cloned.1.call-start = ((), (), s32[]{:S(2)}) async-start(), calls=%async_computation.3 | async-start | bytes 7110656
  18.8 86.6 %copy-start.1 = (f32[788,384]{1,0:T(8,128)}, f32[788,384]{1,0:T(8,128)S(1)}, u32[]{:S(2)}) copy-start(f32[788,384]{1,0:T(8,128)S(1)} %reshape.202) | copy-start | bytes 3631108
  64.3 3.9 copy-start.22
  64.3 3.9 copy-start.26
  86.0 9.9 %copy-start.11 = (bf16[4,197,6,64]{1,3,2,0:T(8,128)(2,1)}, bf16[4,197,6,64]{1,3,2,0:T(8,128)(2,1)S(1)}, u32[]{:S(2)}) copy-start(bf16[4,197,6,64]{1,3,2,0:T(8,128)(2,1)S(1)} %copy.90) | copy-start | bytes 1815556
  107.7 4.7 copy-start.13
  107.7 4.7 copy-start.18
  112.4 16.3 %copy-start.19 = (bf16[384,1536]{1,0:T(8,128)(2,1)S(1)}, bf16[384,1536]{1,0:T(8,128)(2,1)}, u32[]{:S(2)}) copy-start(bf16[384,1536]{1,0:T(8,128)(2,1)} %reshape.209) | copy-start | bytes 3538948
  143.1 5.1 %copy-start.5 = (bf16[4,197,6,64]{1,3,2,0:T(8,128)(2,1)S(1)}, bf16[4,197,6,64]{1,3,2,0:T(8,128)(2,1)}, u32[]{:S(2)}) copy-start(bf16[4,197,6,64]{1,3,2,0:T(8,128)(2,1)} %copy.97) | copy-start | bytes 1815556
  151.3 10.3 %copy-start.12 = (bf16[4,197,6,64]{1,3,2,0:T(8,128)(2,1)S(1)}, bf16[4,197,6,64]{1,3,2,0:T(8,128)(2,1)}, u32[]{:S(2)}) copy-start(bf16[4,197,6,64]{1,3,2,0:T(8,128)(2,1)} %copy.91) | copy-start | bytes 1815556
  181.7 3.7 copy-start.23
  181.7 3.7 copy-start.24
  181.7 3.7 copy-start.25
  193.8 6.6 %copy-start.32 = (bf16[384]{0:T(512)(128)(2,1)S(1)}, bf16[384]{0:T(512)(128)(2,1)}, u32[]{:S(2)}) copy-start(bf16[384]{0:T(512)(128)(2,1)} %get-tuple-element.30) | copy-start | bytes 2308
  193.8 6.6 %copy-start.31 = (bf16[384]{0:T(512)(128)(2,1)S(1)}, bf16[384]{0:T(512)(128)(2,1)}, u32[]{:S(2)}) copy-start(bf16[384]{0:T(512)(128)(2,1)} %get-tuple-element.36) | copy-start | bytes 2308
  193.8 6.6 %copy-start.17 = (bf16[384,384]{1,0:T(8,128)(2,1)S(1)}, bf16[384,384]{1,0:T(8,128)(2,1)}, u32[]{:S(2)}) copy-start(bf16[384,384]{1,0:T(8,128)(2,1)} %convolution_convert_fusion.5) | copy-start | bytes 884740
  202.8 3.8 copy-start.28
  206.7 3.8 copy-start.7
  215.1 205.7 %all-reduce.4.cloned.1.call-start = ((), (), s32[]{:S(2)}) async-start(), calls=%async_computation.1 | async-start | bytes 7110656 | tf_op jit(solution)/shard_map/psum | solution.py:195
  313.5 107.3 %copy-start.20 = (f32[55552]{0:T(1024)S(1)}, f32[55552]{0:T(1024)}, u32[]{:S(2)}) copy-start(f32[55552]{0:T(1024)} %param.8) | copy-start | bytes 666628
  313.5 107.3 %copy-start.21 = (f32[55552]{0:T(1024)S(1)}, f32[55552]{0:T(1024)}, u32[]{:S(2)}) copy-start(f32[55552]{0:T(1024)} %param.9) | copy-start | bytes 666628
  313.5 110.2 %copy-start.30 = (f32[384]{0:T(512)S(1)}, f32[384]{0:T(512)}, u32[]{:S(2)}) copy-start(f32[384]{0:T(512)} %get-tuple-element.48) | copy-start | bytes 4612
  313.5 156.6 %all-gather.6.cloned.1.call-start = ((), (), s32[]{:S(2)}) async-start(), calls=%async_computation.2 | async-start | bytes 3777536 | tf_op jit(solution)/shard_map/all_gather | solution.py:199
  (16 other events, 39.4 us)
Sparse Core Ops, SparseCore 0:
  10.8 52.2 all-gather.3
  215.2 94.7 all-reduce.5
  314.2 106.4 all-reduce.3
  423.8 46.2 all-gather.5
where the time goes:
time: 486 us; the launch traced here: 481 us
  waiting for transfers between devices  283 us (58%)
  local copies, waits for them, and re-layouts  88.2 us (18%)
  matrix products  77.6 us (16%)
  other arithmetic  17.2 us (4%)
  between operations  15.1 us (3%)
    psum x1, waiting for transfers between devices, on_device(): summed_all = lax.psum(half_grad, 'rep')  107 us
    unnamed x5, waiting for transfers between devices  93.7 us
    all_gather x1, waiting for transfers between devices, on_device(): params = unpack(lax.all_gather(half_bf, 'fsdp', axis=0, tiled=True))  44.2 us
    all_gather x1, waiting for transfers between devices, on_device(): new_weights = lax.all_gather(new_own, 'rep', axis=0, tiled=True)  37.5 us
    dot_general x6, matrix products, product(): return jnp.einsum(form, left, right, preferred_element_type=jnp.float32)  32.1 us
    unnamed x86, local copies, waits for them, and re-layouts  20.6 us
    dot_general x1, matrix products, layer_block(): d_act = jnp.dot(d_out, back_fc2.T, preferred_element_type=jnp.float32)  16.3 us
  transfers between devices with their start and end apart: 4, of which 4 were waited for; matrix products, arithmetic and copies ran while one was open for 3% of the time, Pallas kernels for 0%

commit v1 on v0

--- a/solution.py
+++ b/solution.py
@@ -14,6 +14,15 @@
 learn_rate = 0.02
 decay_rate = 0.05
 adam_eps = 1e-08
+
+
+def sum_by_hops(x, axis):
+    size = lax.axis_size(axis)
+    total, far = (x, 1)
+    while far < size:
+        total = total + lax.ppermute(total, axis, [(i, i ^ far) for i in range(size)])
+        far = 2 * far
+    return total
 
 
 def product(form, left, right):
@@ -192,7 +201,7 @@
     ).astype(jnp.float32)
     piece_len = first_moment.shape[0]
     offset = lax.axis_index("rep") * piece_len
-    summed_all = lax.psum(half_grad, "rep")
+    summed_all = sum_by_hops(half_grad, "rep")
     own_grad = lax.dynamic_slice_in_dim(summed_all, offset, piece_len)
     own_weights = lax.dynamic_slice_in_dim(weights, offset, piece_len)
     new_own, new_first, new_second = adamw(own_weights, own_grad, first_moment, second_moment)

time: 486 us -> 699 us (1.44)
  waiting for transfers between devices: 283 us -> 489 us
    ppermute x0 -> x4, waiting for transfers between devices: none -> 312 us  [sum_by_hops(): lax.ppermute(total, axis, [(i, i ^ far) for i in range(size)])]
    psum x1 -> x0, waiting for transfers between devices: 107 us -> none  [on_device(): summed_all = lax.psum(half_grad, 'rep')]
    unnamed x86 -> x88, local copies, waits for them, and re-layouts: 20.6 us -> 20.6 us
    unnamed x5 -> x4, waiting for transfers between devices: 93.7 us -> 93.7 us
  transfers between devices with their start and end apart: 4 -> 7, of which waited for: 4 -> 7; matrix products, arithmetic and copies ran while one was open for 3% -> 2% of each run, Pallas kernels for 0% -> 0%
where the time goes in v1:
time: 699 us; the launch traced here: 694 us
  waiting for transfers between devices  489 us (70%)
  local copies, waits for them, and re-layouts  88.2 us (13%)
  matrix products  77.6 us (11%)
  other arithmetic  18.6 us (3%)
  between operations  15.1 us (2%)
    ppermute x4, waiting for transfers between devices, sum_by_hops(): lax.ppermute(total, axis, [(i, i ^ far) for i in range(size)])  312 us
    unnamed x4, waiting for transfers between devices  93.7 us
    all_gather x1, waiting for transfers between devices, on_device(): params = unpack(lax.all_gather(half_bf, 'fsdp', axis=0, tiled=True))  44.2 us
    all_gather x1, waiting for transfers between devices, on_device(): new_weights = lax.all_gather(new_own, 'rep', axis=0, tiled=True)  38.5 us
    dot_general x6, matrix products, product(): return jnp.einsum(form, left, right, preferred_element_type=jnp.float32)  32.1 us
    unnamed x88, local copies, waits for them, and re-layouts  20.6 us
    dot_general x1, matrix products, layer_block(): d_act = jnp.dot(d_out, back_fc2.T, preferred_element_type=jnp.float32)  16.3 us
  transfers between devices with their start and end apart: 7, of which 7 were waited for; matrix products, arithmetic and copies ran while one was open for 2% of the time, Pallas kernels for 0%

profile of v1, /device:TPU:0, one launch (start us, length us, event | category | flops | bytes accessed | tf_op | source)
XLA Modules:
  0.0 694.0 jit_solution(13055824382537118831)
XLA Ops:
  7.2 3.4 convert_element_type.75
  18.8 44.2 %all-gather.4.cloned.1.call-done = bf16[1777664]{0:T(1024)(128)(2,1)} async-done(((bf16[888832]{0:T(1024)(128)(2,1)}), bf16[1777664]{0:T(1024)(128)(2,1)}) %all-gather.4.cloned.1.call-update) | async-done | bytes 3555344 | tf_op jit(solution)/shard_map/all_gather | solution.py:195
  70.1 2.8 fusion.61
  72.9 3.4 reshape.210
  86.0 3.3 reshape.228
  107.7 4.7 multiply_convert_fusion.1
  112.4 16.3 %fusion.66 = (bf16[1536]{0:T(1024)(128)(2,1)}, bf16[788,1536]{1,0:T(8,128)(2,1)S(1)}) fusion(f32[788,1536]{1,0:T(8,128)S(1)} %get-tuple-element.61, f32[1536]{0:T(1024)S(1)} %slice_convert_fusion.2, bf16[788,384]{1,0:T(8,128)(2,1)S(1)} %copy-done.14, bf16[1536,384]{1,0:T(8,128)(2,1)S(1)} %copy-done.19), kind=kOutput, calls=%fused_computation.108 | convolution fusion | flops 944085504 | bytes 9056256 | tf_op jit(solution)/shard_map/dot_general | solution.py:125
  137.4 3.0 reshape.229
  143.1 5.1 bitcast_convert_fusion
  148.2 3.1 fusion.68
  151.3 10.3 %fusion.31 = bf16[4,197,6,64]{1,3,2,0:T(8,128)(2,1)} fusion(bf16[4,197,6,64]{1,3,2,0:T(8,128)(2,1)} %copy-done.12, f32[4,6,197,197]{2,3,1,0:T(8,128)} %fusion.68, f32[4,6,197,197]{2,3,1,0:T(8,128)} %copy-done, f32[4,6,197]{2,1,0:T(8,128)S(1)} %log_add_fusion), kind=kOutput, calls=%fused_computation.39 | convolution fusion | flops 127911504 | bytes 8680608 | tf_op jit(solution)/shard_map/bhqk,bqhd->bkhd/dot_general | solution.py:29
  161.6 10.5 %bitcast_convert_fusion.1 = (bf16[4,197,6,64]{1,3,2,0:T(8,128)(2,1)}, f32[4,6,64,197]{3,2,1,0:T(8,128)}) fusion(bf16[4,197,6,64]{1,3,2,0:T(8,128)(2,1)S(1)} %copy-done.13, f32[4,6,197,197]{2,3,1,0:T(8,128)} %fusion.68, f32[4,6,197,197]{2,3,1,0:T(8,128)} %copy-done, f32[4,6,197]{2,1,0:T(8,128)S(1)} %log_add_fusion), kind=kOutput, calls=%fused_computation.29 | convolution fusion | flops 127911504 | bytes 9890976 | tf_op jit(solution)/shard_map/bhqk,bkhd->bqhd/dot_general | solution.py:29
  185.5 2.8 multiply_reduce_fusion.3
  190.9 2.8 convolution_convert_fusion
  193.8 3.1 reshape.221
  196.9 3.5 reshape.220
  216.4 93.6 %all-reduce.3.cloned.1.call-done = bf16[1777664]{0:T(1024)(128)(2,1)} async-done(((bf16[1777664]{0:T(1024)(128)(2,1)}), bf16[1777664]{0:T(1024)(128)(2,1)}) %all-reduce.3.cloned.1.call-update) | async-done | bytes 3555344
  311.9 6.2 collective-permute-done
  320.0 77.4 %collective-permute-done.1 = f32[888832]{0:T(1024)S(1)} collective-permute-done((f32[888832]{0:T(1024)S(1)}, f32[888832]{0:T(1024)S(1)}, u32[]{:S(2)}, u32[]{:S(2)}) %collective-permute-start.1) | collective-permute-done | bytes 3555360 | tf_op jit(solution)/shard_map/ppermute | solution.py:23
  399.4 76.6 %collective-permute-done.2 = f32[888832]{0:T(1024)S(1)} collective-permute-done((f32[888832]{0:T(1024)S(1)}, f32[888832]{0:T(1024)S(1)}, u32[]{:S(2)}, u32[]{:S(2)}) %collective-permute-start.2) | collective-permute-done | bytes 3555360 | tf_op jit(solution)/shard_map/ppermute | solution.py:23
  480.5 152.2 %collective-permute-done.3 = f32[888832]{0:T(1024)} collective-permute-done((f32[888832]{0:T(1024)}, f32[888832]{0:T(1024)}, u32[]{:S(2)}, u32[]{:S(2)}) %collective-permute-start.3) | collective-permute-done | bytes 3555360 | tf_op jit(solution)/shard_map/ppermute | solution.py:23
  635.9 4.3 fusion.29
  644.8 38.5 %all-gather.6.cloned.1.call-done = f32[16,1,55552]{2,1,0:T(1,128)} async-done(((f32[1,1,55552]{2,1,0:T(1,128)}), f32[16,1,55552]{2,1,0:T(1,128)}) %all-gather.6.cloned.1.call-update) | async-done | bytes 3555344 | tf_op jit(solution)/shard_map/all_gather | solution.py:208
  683.3 4.0 copy.134
  (178 shorter events, 103.6 us)
Async XLA Ops:
  7.2 55.9 %all-gather.4.cloned.1.call-start = ((), (), s32[]{:S(2)}) async-start(), calls=%async_computation | async-start | bytes 5332992 | tf_op jit(solution)/shard_map/all_gather | solution.py:195
  10.6 299.4 %all-reduce.3.cloned.1.call-start = ((), (), s32[]{:S(2)}) async-start(), calls=%async_computation.2 | async-start | bytes 7110656
  18.8 86.6 %copy-start.1 = (f32[788,384]{1,0:T(8,128)}, f32[788,384]{1,0:T(8,128)S(1)}, u32[]{:S(2)}) copy-start(f32[788,384]{1,0:T(8,128)S(1)} %reshape.202) | copy-start | bytes 3631108
  64.3 3.9 copy-start.23
  64.3 3.9 copy-start.27
  86.0 9.9 %copy-start.12 = (bf16[4,197,6,64]{1,3,2,0:T(8,128)(2,1)}, bf16[4,197,6,64]{1,3,2,0:T(8,128)(2,1)S(1)}, u32[]{:S(2)}) copy-start(bf16[4,197,6,64]{1,3,2,0:T(8,128)(2,1)S(1)} %copy.90) | copy-start | bytes 1815556
  107.7 4.7 copy-start.14
  107.7 4.7 copy-start.19
  112.4 16.3 %copy-start.20 = (bf16[384,1536]{1,0:T(8,128)(2,1)S(1)}, bf16[384,1536]{1,0:T(8,128)(2,1)}, u32[]{:S(2)}) copy-start(bf16[384,1536]{1,0:T(8,128)(2,1)} %reshape.209) | copy-start | bytes 3538948
  143.1 5.1 copy-start.5
  151.3 10.3 %copy-start.13 = (bf16[4,197,6,64]{1,3,2,0:T(8,128)(2,1)S(1)}, bf16[4,197,6,64]{1,3,2,0:T(8,128)(2,1)}, u32[]{:S(2)}) copy-start(bf16[4,197,6,64]{1,3,2,0:T(8,128)(2,1)} %copy.91) | copy-start | bytes 1815556
  193.8 6.6 copy-start.33
  193.8 6.6 copy-start.32
  193.8 6.6 copy-start.18
  202.8 3.8 copy-start.29
  215.1 468.2 %all-gather.6.cloned.1.call-start = ((), (), s32[]{:S(2)}) async-start(), calls=%async_computation.1 | async-start | bytes 3777536 | tf_op jit(solution)/shard_map/all_gather | solution.py:208
  310.0 8.2 %copy-start.9 = (bf16[1777664]{0:T(1024)(128)(2,1)S(1)}, bf16[1777664]{0:T(1024)(128)(2,1)}, u32[]{:S(2)}) copy-start(bf16[1777664]{0:T(1024)(128)(2,1)} %all-reduce.3.cloned.1.call-done) | copy-start | bytes 10665988
  311.8 6.3 collective-permute-start
  318.5 79.0 %collective-permute-start.1 = (f32[888832]{0:T(1024)S(1)}, f32[888832]{0:T(1024)S(1)}, u32[]{:S(2)}, u32[]{:S(2)}) collective-permute-start(f32[888832]{0:T(1024)S(1)} %fusion.39), channel_id=1, source_target_pairs={{0,2},{1,3},{2,0},{3,1},{4,6},{5,7},{6,4},{7,5},{8,10},{9,11},{10,... | collective-permute-start | bytes 10665992 | tf_op jit(solution)/shard_map/ppermute | solution.py:23
  397.8 234.9 %copy-start.21 = (f32[55552]{0:T(1024)S(1)}, f32[55552]{0:T(1024)}, u32[]{:S(2)}) copy-start(f32[55552]{0:T(1024)} %param.8) | copy-start | bytes 666628
  397.8 234.9 %copy-start.22 = (f32[55552]{0:T(1024)S(1)}, f32[55552]{0:T(1024)}, u32[]{:S(2)}) copy-start(f32[55552]{0:T(1024)} %param.9) | copy-start | bytes 666628
  397.8 78.1 %collective-permute-start.2 = (f32[888832]{0:T(1024)S(1)}, f32[888832]{0:T(1024)S(1)}, u32[]{:S(2)}, u32[]{:S(2)}) collective-permute-start(f32[888832]{0:T(1024)S(1)} %add.169), channel_id=1, source_target_pairs={{0,4},{1,5},{2,6},{3,7},{4,0},{5,1},{6,2},{7,3},{8,12},{9,13},{10,... | collective-permute-start | bytes 10665992 | tf_op jit(solution)/shard_map/ppermute | solution.py:23
  478.1 157.8 %copy-start.31 = (f32[384]{0:T(512)S(1)}, f32[384]{0:T(512)}, u32[]{:S(2)}) copy-start(f32[384]{0:T(512)} %get-tuple-element.48) | copy-start | bytes 4612
  478.1 154.6 %collective-permute-start.3 = (f32[888832]{0:T(1024)}, f32[888832]{0:T(1024)}, u32[]{:S(2)}, u32[]{:S(2)}) collective-permute-start(f32[888832]{0:T(1024)} %add.170), channel_id=1, source_target_pairs={{0,8},{1,9},{2,10},{3,11},{4,12},{5,13},{6,14},{7,15},{8,0},{9,1},... | collective-permute-start | bytes 10665992 | tf_op jit(solution)/shard_map/ppermute | solution.py:23
  (20 other events, 54.4 us)
Sparse Core Ops, SparseCore 0:
  10.8 52.2 all-gather.3
  215.2 94.7 all-reduce.2
  636.0 47.2 all-gather.5
